TPU v7x, 512 devices: a whole 4x4x16 slice. The times are simulated.
512 devices in a mesh: dp: 32 (over z, x_lo), fsdp: 16 (over y, x_hi, core).
Axes of the slice: x: 4 (x_hi: 2, x_lo: 2; x = x_hi * 2 + x_lo), y: 4, z: 16, core: 2. Of those that a mesh axis runs over, the one named last changes fastest.
Arguments:
- images: bfloat16 [1024, 8, 8, 3072], P(('dp', 'fsdp')), may hold values from -6 to 6
- dw_weight: float32 [49, 3072], P(None, 'fsdp'), may hold values from -0.875 to 0.875
- dw_bias: float32 [3072], P('fsdp'), may hold values from -1 to 1
- block_gain: float32 [3072], P('fsdp'), may hold values from 0.5 to 1.5
- head_gain: float32 [3072], P('fsdp'), may hold values from 0.5 to 1.5
- projection: bfloat16 [3072, 512], P('fsdp'), may hold values from -0.109375 to 0.109375
- text: bfloat16 [1024, 512], P(('dp', 'fsdp')), may hold values from -6 to 6
Outputs:
- loss: float32 [], replicated
- grad_images: bfloat16 [1024, 8, 8, 3072], P(('dp', 'fsdp'))
- grad_dw_weight: float32 [49, 3072], P(None, 'fsdp')
- grad_dw_bias: float32 [3072], P('fsdp')
- grad_block_gain: float32 [3072], P('fsdp')
- grad_head_gain: float32 [3072], P('fsdp')
- grad_projection: float32 [3072, 512], P('fsdp')
- grad_text: float32 [1024, 512], P(('dp', 'fsdp'))
All inputs are finite; a program needn't handle non-finite values.
Results may differ from a plain program's by a relative error of at most 0.012.
Values may be sent and summed in bfloat16 or wider, within the bound.
A program may use at most 64 MiB of HBM per device.

v0:
```python
import jax
import jax.numpy as jnp
from jax import lax
from jax.sharding import PartitionSpec as P

KERNEL = 7
MAP_SIDE = 8
LOGIT_SCALE = 14.0
EPSILON = 1e-06


def depthwise(padded, weight):
    total = jnp.zeros(padded.shape[:1] + (MAP_SIDE, MAP_SIDE, padded.shape[3]), jnp.float32)
    for tap_row in range(KERNEL):
        for tap_col in range(KERNEL):
            window = padded[:, tap_row : tap_row + MAP_SIDE, tap_col : tap_col + MAP_SIDE, :]
            total = total + window * weight[tap_row * KERNEL + tap_col]
    return total


def contract(left, right, left_dim, right_dim):
    return lax.dot_general(
        left, right, (((left_dim,), (right_dim,)), ((), ())), preferred_element_type=jnp.float32
    )


def local(images, dw_weight, dw_bias, block_gain, head_gain, projection, text):
    full_weight, full_bias, full_block, full_head = (
        lax.all_gather(dw_weight, "fsdp", axis=1, tiled=True),
        lax.all_gather(dw_bias, "fsdp", axis=0, tiled=True),
        lax.all_gather(block_gain, "fsdp", axis=0, tiled=True),
        lax.all_gather(head_gain, "fsdp", axis=0, tiled=True),
    )
    margin = KERNEL // 2
    as_float = images.astype(jnp.float32)
    padded = jnp.pad(as_float, ((0, 0), (margin, margin), (margin, margin), (0, 0)))
    conv_out = depthwise(padded, full_weight) + full_bias
    centred = conv_out - jnp.mean(conv_out, axis=3, keepdims=True)
    inverse = lax.rsqrt(jnp.mean(centred * centred, axis=3, keepdims=True) + EPSILON)
    normal_z = centred * inverse
    hidden = as_float + normal_z * full_block
    pooled = jnp.mean(hidden, axis=(1, 2))
    pool_centred = pooled - jnp.mean(pooled, axis=1, keepdims=True)
    pool_inverse = lax.rsqrt(jnp.mean(pool_centred * pool_centred, axis=1, keepdims=True) + EPSILON)
    pool_normed = pool_centred * pool_inverse
    query = (pool_normed * full_head).astype(jnp.bfloat16)
    query_parts = lax.all_to_all(query, "fsdp", split_axis=1, concat_axis=0, tiled=True)
    panels = lax.all_gather(projection, "fsdp", axis=0, tiled=True)
    embedding = jnp.dot(query, panels, preferred_element_type=jnp.float32)
    image_scale = lax.rsqrt(jnp.sum(embedding * embedding, axis=1, keepdims=True) + EPSILON)
    image_f = embedding * image_scale
    image_unit = image_f.astype(jnp.bfloat16)
    text_float = text.astype(jnp.float32)
    text_scale = lax.rsqrt(jnp.sum(text_float * text_float, axis=1, keepdims=True) + EPSILON)
    text_f = text_float * text_scale
    text_unit = text_f.astype(jnp.bfloat16)
    image_all, text_all = (
        lax.all_gather(image_unit, ("dp", "fsdp"), axis=0, tiled=True),
        lax.all_gather(text_unit, ("dp", "fsdp"), axis=0, tiled=True),
    )
    local_count = images.shape[0]
    offset = lax.axis_index(("dp", "fsdp")) * local_count
    row_logits = LOGIT_SCALE * contract(image_unit, text_all, 1, 1)
    col_logits = LOGIT_SCALE * contract(image_all, text_unit, 1, 1)
    row_lse = jnp.log(jnp.sum(jnp.exp(row_logits), axis=1))
    col_lse = jnp.log(jnp.sum(jnp.exp(col_logits), axis=0))
    diagonal = LOGIT_SCALE * jnp.sum(
        image_unit.astype(jnp.float32) * text_unit.astype(jnp.float32), axis=1
    )
    every_row, every_col, every_diag = (
        lax.all_gather(row_lse, ("dp", "fsdp"), axis=0, tiled=True),
        lax.all_gather(col_lse, ("dp", "fsdp"), axis=0, tiled=True),
        lax.all_gather(diagonal, ("dp", "fsdp"), axis=0, tiled=True),
    )
    total_pairs = every_row.shape[0]
    loss = (jnp.sum(every_row) + jnp.sum(every_col) - 2.0 * jnp.sum(every_diag)) / (
        2.0 * total_pairs
    )
    positions = jnp.arange(total_pairs, dtype=jnp.int32)
    owners = offset + jnp.arange(local_count, dtype=jnp.int32)
    onehot = (positions[None, :] == owners[:, None]).astype(jnp.float32)
    row_weights = (
        jnp.exp(row_logits - row_lse[:, None])
        + jnp.exp(row_logits - every_col[None, :])
        - 2.0 * onehot
    ).astype(jnp.bfloat16)
    col_weights = (
        jnp.exp(col_logits - every_row[:, None])
        + jnp.exp(col_logits - col_lse[None, :])
        - 2.0 * onehot.T
    ).astype(jnp.bfloat16)
    d_image = 7.0 * jnp.dot(row_weights, text_all, preferred_element_type=jnp.float32)
    d_caption = 7.0 * contract(col_weights, image_all, 0, 0)
    d_embedding = (
        image_scale * (d_image - image_f * jnp.sum(image_f * d_image, axis=1, keepdims=True))
    ).astype(jnp.bfloat16)
    grad_text = text_scale * (
        d_caption - text_f * jnp.sum(text_f * d_caption, axis=1, keepdims=True)
    )
    demb_group = lax.all_gather(d_embedding, "fsdp", axis=0, tiled=True)
    proj_grad = contract(query_parts, demb_group, 0, 0)
    d_query = contract(d_embedding, panels, 1, 1)
    d_normed = d_query * full_head
    g_head = jnp.sum(d_query * pool_normed, axis=0)
    d_pooled = pool_inverse * (
        d_normed
        - jnp.mean(d_normed, axis=1, keepdims=True)
        - pool_normed * jnp.mean(d_normed * pool_normed, axis=1, keepdims=True)
    )
    d_hidden = (d_pooled / float(MAP_SIDE * MAP_SIDE))[:, None, None, :]
    d_norm = d_hidden * full_block
    g_block = jnp.sum(d_hidden * normal_z, axis=(0, 1, 2))
    d_conv = inverse * (
        d_norm
        - jnp.mean(d_norm, axis=3, keepdims=True)
        - normal_z * jnp.mean(d_norm * normal_z, axis=3, keepdims=True)
    )
    g_bias = jnp.sum(d_conv, axis=(0, 1, 2))
    d_padded = jnp.pad(d_conv, ((0, 0), (margin, margin), (margin, margin), (0, 0)))
    tap_grads = []
    d_images = d_hidden + jnp.zeros_like(d_conv)
    for tap_row in range(KERNEL):
        for tap_col in range(KERNEL):
            window = padded[:, tap_row : tap_row + MAP_SIDE, tap_col : tap_col + MAP_SIDE, :]
            tap_grads.append(jnp.sum(d_conv * window, axis=(0, 1, 2)))
            back = d_padded[
                :,
                2 * margin - tap_row : 2 * margin - tap_row + MAP_SIDE,
                2 * margin - tap_col : 2 * margin - tap_col + MAP_SIDE,
                :,
            ]
            d_images = d_images + back * full_weight[tap_row * KERNEL + tap_col]
    g_weight = jnp.stack(tap_grads)
    part_weight, part_bias, part_block, part_head = (
        lax.psum_scatter(g_weight, "fsdp", scatter_dimension=1, tiled=True),
        lax.psum_scatter(g_bias, "fsdp", scatter_dimension=0, tiled=True),
        lax.psum_scatter(g_block, "fsdp", scatter_dimension=0, tiled=True),
        lax.psum_scatter(g_head, "fsdp", scatter_dimension=0, tiled=True),
    )
    sum_weight, sum_bias, sum_block, sum_head, sum_proj = lax.psum(
        (part_weight, part_bias, part_block, part_head, proj_grad), "dp"
    )
    return (
        loss,
        d_images.astype(jnp.bfloat16),
        sum_weight,
        sum_bias,
        sum_block,
        sum_head,
        sum_proj,
        grad_text,
    )


def solution(mesh):
    return jax.shard_map(
        local,
        mesh=mesh,
        in_specs=(
            P(("dp", "fsdp"), None, None, None),
            P(None, "fsdp"),
            P("fsdp"),
            P("fsdp"),
            P("fsdp"),
            P("fsdp", None),
            P(("dp", "fsdp"), None),
        ),
        out_specs=(
            P(),
            P(("dp", "fsdp"), None, None, None),
            P(None, "fsdp"),
            P("fsdp"),
            P("fsdp"),
            P("fsdp"),
            P("fsdp", None),
            P(("dp", "fsdp"), None),
        ),
        check_vma=False,
    )
```

profile of v0, /device:TPU:4, one launch (start us, length us, event | category | flops | bytes accessed | tf_op | source)
XLA Modules:
  0.0 2228.4 jit_solution(11575561516436154558)
XLA Ops:
  7.2 0.7 all-gather.8.cloned.1.call-update
  8.0 28.4 %all-gather = f32[16,192,49]{1,2,0:T(8,128)S(1)} all-gather(f32[1,192,49]{1,2,0:T(8,128)} %bitcast.227), channel_id=1, replica_groups=mesh['dp'=32,'fsdp'=16] {'fsdp'}, dimensions={0}, use_global_device_ids=true | all-gather | bytes 639744 | tf_op jit(solution)/shard_map/all_gather | solution.py:29
  36.4 0.3 copy.21
  36.7 1.2 reshape.181
  37.9 0.1 convert_element_type.41
  38.1 0.6 fusion.135
  39.4 0.3 dynamic-update-slice
  39.6 0.3 dynamic-update-slice.1
  39.9 0.3 dynamic-update-slice.2
  40.2 62.7 %all-reduce.14 = (f32[3072]{0:T(1024)}, f32[3072]{0:T(1024)}, f32[3072]{0:T(1024)S(1)}) all-reduce(f32[3072]{0:T(1024)S(1)} %dynamic-update-slice, f32[3072]{0:T(1024)S(1)} %dynamic-update-slice.1, f32[3072]{0:T(1024)S(1)} %dynamic-update-slice.2), channel_id=1, replica_groups=mesh['dp'=32,'fsdp'=16] {'fsdp'}, use_global_device_ids=true, to_apply=%add.2 | all-reduce | flops 9216 | bytes 73728
  103.1 0.2 fusion.133
  103.4 0.2 fusion.132
  103.7 14.5 fusion.131
  118.5 0.3 multiply_reduce_fusion.51
  118.8 0.8 copy-done.3
  119.6 0.5 add_reduce_fusion
  120.1 0.7 broadcast_multiply_fusion.2
  120.8 0.2 multiply_reduce_fusion.54
  121.1 2.6 multiply_reduce_fusion.58
  123.7 1.3 multiply_reduce_fusion.57
  125.0 0.7 all-gather.10.cloned.1.call-update
  125.7 0.7 mul.1444
  126.4 0.8 div.46
  127.2 0.8 multiply_convert_fusion
  128.0 0.6 copy.22
  128.6 9.2 all-to-all-start
  137.9 1.3 broadcast_multiply_fusion.3
  139.2 0.5 iota_add_fusion
  140.3 2.3 all-to-all-done
  142.6 0.6 all_to_all.14
  143.2 0.7 multiply_dynamic-update-slice_fusion
  144.0 749.1 %all-gather.12.cloned.1.call-done = bf16[512,2,512]{2,1,0:T(2,128)(2,1)} async-done(((bf16[1,2,512]{2,1,0:T(2,128)(2,1)}), bf16[512,2,512]{2,1,0:T(2,128)(2,1)}) %all-gather.12.cloned.1.call-update) | async-done | bytes 1048592 | tf_op jit(solution)/shard_map/all_gather | solution.py:58
  893.1 2.3 reshape.185
  895.3 2.3 exponential_reduce_fusion
  897.7 756.2 %all-gather.10.cloned.1.call-done = bf16[512,2,512]{2,1,0:T(2,128)(2,1)} async-done(((bf16[1,2,512]{2,1,0:T(2,128)(2,1)}), bf16[512,2,512]{2,1,0:T(2,128)(2,1)}) %all-gather.10.cloned.1.call-update) | async-done | bytes 1048592 | tf_op jit(solution)/shard_map/all_gather | solution.py:59
  1653.8 2.3 reshape.183
  1656.1 1.7 exponential_reduce_fusion.1
  1657.8 0.6 fusion.136
  1658.4 0.5 fusion.137
  1658.9 101.7 %all-reduce.11 = (f32[1024]{0:T(1024)}, f32[1024]{0:T(1024)S(1)}, f32[1024]{0:T(1024)}) all-reduce(f32[1024]{0:T(1024)S(1)} %get-tuple-element.153, f32[1024]{0:T(1024)S(1)} %get-tuple-element.151, f32[1024]{0:T(1024)S(1)} %multiply_dynamic-update-slice_fusion), channel_id=1, replica_groups=mesh['dp'=32,'fsdp'=16] {'dp','fsdp'}, use_global_device_ids=true, to_apply=%add.5 | all-reduce | flops 3072 | bytes 24576
  1760.6 1.7 multiply_reduce_fusion.56
  1762.3 0.7 multiply_convert_fusion.3
  1763.1 3.4 multiply_reduce_fusion.52
  1766.5 0.2 fusion.129
  1766.8 1.1 multiply_reduce_fusion
  1767.9 4.7 multiply_reduce_fusion.1
  1772.6 2.4 fusion.128
  1775.2 3.8 multiply_reduce_fusion.19
  1779.1 21.1 all-gather.3
  1800.2 62.4 %all-reduce.13 = (f32[3072]{0:T(1024)S(1)}, f32[3072]{0:T(1024)S(1)}, f32[3072]{0:T(1024)S(1)}) all-reduce(f32[3072]{0:T(1024)S(1)} %get-tuple-element.58, f32[3072]{0:T(1024)S(1)} %copy-done.73, f32[3072]{0:T(1024)S(1)} %copy-done.72), channel_id=3, replica_groups=mesh['dp'=32,'fsdp'=16] {'fsdp'}, use_global_device_ids=true, to_apply=%region_70.71.clone | all-reduce | flops 9216 | bytes 73728
  1863.0 0.9 stack.199
  1863.9 1.7 copy.23
  1865.9 1.4 reduce_sum.649
  1867.3 1.0 fusion.138
  1868.6 9.5 fusion.97
  1878.1 0.6 reduce_sum.647
  1880.0 0.6 reduce_sum.651
  1881.4 0.4 fusion.113
  1881.8 0.7 fusion.115
  1882.4 70.2 %reduce-scatter.4.cloned.1.call-done = f32[192,49]{1,0:T(8,128)} async-done(((f32[3072,49]{1,0:T(8,128)}), f32[192,49]{1,0:T(8,128)}) %reduce-scatter.4.cloned.1.call-update) | async-done | bytes 37648
  1952.7 1.0 copy.24
  1953.7 123.0 %all-reduce.12 = (f32[49,192]{1,0:T(8,128)}, f32[192]{0:T(256)}, f32[192]{0:T(256)}, f32[192]{0:T(256)}) all-reduce(f32[49,192]{1,0:T(8,128)S(1)} %copy.24, f32[192]{0:T(256)S(1)} %dynamic-slice.4, f32[192]{0:T(256)S(1)} %dynamic-slice.6, f32[192]{0:T(256)S(1)} %dynamic-slice.8), channel_id=1, replica_groups=mesh['dp'=32,'fsdp'=16] {'dp'}, use_global_device_ids=true, to_apply=%region_68.69 | all-reduce | flops 9984 | bytes 79872 | tf_op jit(solution)/shard_map/psum | solution.py:140
  2076.7 142.3 %all-reduce.17.cloned.1.call-done = f32[192,512]{1,0:T(8,128)} async-done(((f32[192,512]{1,0:T(8,128)}), f32[192,512]{1,0:T(8,128)}) %all-reduce.17.cloned.1.call-update) | async-done | bytes 393232 | tf_op jit(solution)/shard_map/psum | solution.py:140
  2219.0 1.8 copy.35
  (223 shorter events, 1.3 us)
Async XLA Ops:
  7.2 113.9 %all-gather.8.cloned.1.call-start = ((), (), s32[]{:S(2)}) async-start(), calls=%async_computation.2 | async-start | bytes 3342336 | tf_op jit(solution)/shard_map/all_gather | solution.py:48
  7.9 885.2 %all-gather.12.cloned.1.call-start = ((), (), s32[]{:S(2)}) async-start(), calls=%async_computation.5 | async-start | bytes 1050624 | tf_op jit(solution)/shard_map/all_gather | solution.py:58
  37.9 65.0 %copy-start.77 = (bf16[2,512]{1,0:T(2,128)(2,1)S(1)}, bf16[2,512]{1,0:T(2,128)(2,1)}, u32[]{:S(2)}) copy-start(bf16[2,512]{1,0:T(2,128)(2,1)} %param.13) | copy-start | bytes 6148
  37.9 65.1 %copy-start.6 = (f32[3072,49]{0,1:T(8,128)S(1)}, f32[3072,49]{0,1:T(8,128)}, u32[]{:S(2)}) copy-start(f32[3072,49]{0,1:T(8,128)} %reshape.181) | copy-start | bytes 1806340
  103.3 14.9 copy-start.7
  103.3 14.9 copy-start.9
  103.3 14.9 copy-start.11
  103.3 14.9 copy-start.13
  103.5 14.7 copy-start.15
  103.5 14.7 copy-start.17
  103.5 14.7 copy-start.19
  103.6 14.7 copy-start.21
  103.6 14.7 copy-start.23
  103.6 14.7 copy-start.25
  103.6 14.7 copy-start.27
  103.6 14.7 copy-start.29
  103.6 14.7 copy-start.31
  103.6 14.7 copy-start.33
  103.6 14.7 copy-start.35
  103.6 14.7 copy-start.37
  103.6 14.7 copy-start.39
  103.7 14.7 copy-start.41
  103.7 14.7 copy-start.43
  103.7 14.7 copy-start.45
  103.7 14.7 copy-start.47
  103.7 14.7 copy-start.49
  103.7 14.7 copy-start.51
  125.0 1528.8 %all-gather.10.cloned.1.call-start = ((), (), s32[]{:S(2)}) async-start(), calls=%async_computation.4 | async-start | bytes 1050624 | tf_op jit(solution)/shard_map/all_gather | solution.py:59
  128.0 767.3 %copy-start.76 = (bf16[2,512]{1,0:T(2,128)(2,1)S(1)}, bf16[2,512]{1,0:T(2,128)(2,1)}, u32[]{:S(2)}) copy-start(bf16[2,512]{1,0:T(2,128)(2,1)} %get-tuple-element.93) | copy-start | bytes 6148
  128.6 14.0 all-to-all-start
  137.8 1814.9 %reduce-scatter.4.cloned.1.call-start = ((), (), s32[]{:S(2)}) async-start(), calls=%async_computation.6 | async-start | bytes 1671168
  895.3 760.8 %copy-start.75 = (bf16[2,512]{1,0:T(2,128)(2,1)S(1)}, bf16[2,512]{1,0:T(2,128)(2,1)}, u32[]{:S(2)}) copy-start(bf16[2,512]{1,0:T(2,128)(2,1)} %get-tuple-element.94) | copy-start | bytes 6148
  1656.1 107.0 %copy-start.80 = (f32[2]{0:T(128)S(1)}, f32[2]{0:T(128)}, u32[]{:S(2)}) copy-start(f32[2]{0:T(128)} %copy-done.79) | copy-start | bytes 28
  1656.1 107.0 %copy-start.83 = (f32[2]{0:T(128)S(1)}, f32[2]{0:T(128)}, u32[]{:S(2)}) copy-start(f32[2]{0:T(128)} %copy-done.82) | copy-start | bytes 28
  1763.0 3.5 copy-start.74
  1767.9 4.8 copy-start.4
  1775.0 25.2 %copy-start.72 = (f32[3072]{0:T(1024)S(1)}, f32[3072]{0:T(1024)}, u32[]{:S(2)}) copy-start(f32[3072]{0:T(1024)} %get-tuple-element.72) | copy-start | bytes 36868
  1775.0 25.1 %copy-start.73 = (f32[3072]{0:T(1024)S(1)}, f32[3072]{0:T(1024)}, u32[]{:S(2)}) copy-start(f32[3072]{0:T(1024)} %get-tuple-element.56) | copy-start | bytes 36868
  1775.1 87.8 %copy-start.54 = (f32[3072]{0:T(1024)S(1)}, f32[3072]{0:T(1024)}, u32[]{:S(2)}) copy-start(f32[3072]{0:T(1024)} %get-tuple-element.9) | copy-start | bytes 36868
  1775.1 87.8 %copy-start.55 = (f32[3072]{0:T(1024)S(1)}, f32[3072]{0:T(1024)}, u32[]{:S(2)}) copy-start(f32[3072]{0:T(1024)} %get-tuple-element.10) | copy-start | bytes 36868
  1775.1 87.8 %copy-start.56 = (f32[3072]{0:T(1024)S(1)}, f32[3072]{0:T(1024)}, u32[]{:S(2)}) copy-start(f32[3072]{0:T(1024)} %get-tuple-element.11) | copy-start | bytes 36868
  1775.1 87.8 %copy-start.57 = (f32[3072]{0:T(1024)S(1)}, f32[3072]{0:T(1024)}, u32[]{:S(2)}) copy-start(f32[3072]{0:T(1024)} %get-tuple-element.12) | copy-start | bytes 36868
  1775.1 87.8 %copy-start.58 = (f32[3072]{0:T(1024)S(1)}, f32[3072]{0:T(1024)}, u32[]{:S(2)}) copy-start(f32[3072]{0:T(1024)} %get-tuple-element.13) | copy-start | bytes 36868
  1775.1 87.8 %copy-start.59 = (f32[3072]{0:T(1024)S(1)}, f32[3072]{0:T(1024)}, u32[]{:S(2)}) copy-start(f32[3072]{0:T(1024)} %get-tuple-element.14) | copy-start | bytes 36868
  1775.1 87.8 %copy-start.60 = (f32[3072]{0:T(1024)S(1)}, f32[3072]{0:T(1024)}, u32[]{:S(2)}) copy-start(f32[3072]{0:T(1024)} %get-tuple-element.15) | copy-start | bytes 36868
  1775.1 87.8 %copy-start.61 = (f32[3072]{0:T(1024)S(1)}, f32[3072]{0:T(1024)}, u32[]{:S(2)}) copy-start(f32[3072]{0:T(1024)} %get-tuple-element.16) | copy-start | bytes 36868
  1775.1 87.8 %copy-start.62 = (f32[3072]{0:T(1024)S(1)}, f32[3072]{0:T(1024)}, u32[]{:S(2)}) copy-start(f32[3072]{0:T(1024)} %get-tuple-element.17) | copy-start | bytes 36868
  1775.1 87.8 %copy-start.63 = (f32[3072]{0:T(1024)S(1)}, f32[3072]{0:T(1024)}, u32[]{:S(2)}) copy-start(f32[3072]{0:T(1024)} %get-tuple-element.18) | copy-start | bytes 36868
  1775.2 87.8 %copy-start.64 = (f32[3072]{0:T(1024)S(1)}, f32[3072]{0:T(1024)}, u32[]{:S(2)}) copy-start(f32[3072]{0:T(1024)} %get-tuple-element.19) | copy-start | bytes 36868
  1775.2 87.8 %copy-start.65 = (f32[3072]{0:T(1024)S(1)}, f32[3072]{0:T(1024)}, u32[]{:S(2)}) copy-start(f32[3072]{0:T(1024)} %get-tuple-element.20) | copy-start | bytes 36868
  1775.2 87.8 %copy-start.66 = (f32[3072]{0:T(1024)S(1)}, f32[3072]{0:T(1024)}, u32[]{:S(2)}) copy-start(f32[3072]{0:T(1024)} %get-tuple-element.21) | copy-start | bytes 36868
  1775.2 87.8 %copy-start.67 = (f32[3072]{0:T(1024)S(1)}, f32[3072]{0:T(1024)}, u32[]{:S(2)}) copy-start(f32[3072]{0:T(1024)} %get-tuple-element.22) | copy-start | bytes 36868
  1775.2 87.8 %copy-start.68 = (f32[3072]{0:T(1024)S(1)}, f32[3072]{0:T(1024)}, u32[]{:S(2)}) copy-start(f32[3072]{0:T(1024)} %get-tuple-element.23) | copy-start | bytes 36868
  1775.2 87.8 %copy-start.69 = (f32[3072]{0:T(1024)S(1)}, f32[3072]{0:T(1024)}, u32[]{:S(2)}) copy-start(f32[3072]{0:T(1024)} %get-tuple-element.24) | copy-start | bytes 36868
  1775.2 87.8 %copy-start.70 = (f32[3072]{0:T(1024)S(1)}, f32[3072]{0:T(1024)}, u32[]{:S(2)}) copy-start(f32[3072]{0:T(1024)} %get-tuple-element.25) | copy-start | bytes 36868
  1865.8 353.2 %all-reduce.17.cloned.1.call-start = ((), (), s32[]{:S(2)}) async-start(), calls=%async_computation.3 | async-start | bytes 786432 | tf_op jit(solution)/shard_map/psum | solution.py:140
  1868.5 9.6 copy-start.84
  1868.5 11.5 copy-start.85
  1868.5 12.8 copy-start.5
  1868.5 12.8 copy-start.78
  1868.5 12.8 copy-start.81
  1868.6 12.8 copy-start.88
  1868.6 12.8 copy-start.94
  1868.6 12.8 copy-start.95
  (38 other events, 94.8 us)
Sparse Core Ops, SparseCore 0:
  11.3 68.0 all-gather.7
  125.1 767.9 all-gather.11
  895.8 758.0 all-gather.9
  1865.9 86.6 reduce-scatter.3
  1956.0 262.9 all-reduce.16
where the time goes:
time: 2230 us
  waiting for transfers between devices  1720 us (77%)
  blocking collectives  399 us (18%)
  other arithmetic  47 us (2%)
    all_gather x1, waiting for transfers between devices, local(): lax.all_gather(text_unit, ('dp', 'fsdp'), axis=0, tiled=True)  756 us
    all_gather x1, waiting for transfers between devices, local(): lax.all_gather(image_unit, ('dp', 'fsdp'), axis=0, tiled=True)  749 us
    unnamed x3, blocking collectives  227 us
    psum x1, waiting for transfers between devices, local(): lax.psum((part_weight, part_bias, part_block, part_head, proj_grad), 'dp')  142 us
    psum x1, blocking collectives, local(): lax.psum((part_weight, part_bias, part_block, part_head, proj_grad), 'dp')  123 us
    unnamed x6, waiting for transfers between devices  71.6 us
  transfers between devices with their start and end apart: 6, of which 5 were waited for; matrix products, arithmetic and copies ran while one was open for 2% of the time, Pallas kernels for 0%

commit v1 on v0

--- a/solution.py
+++ b/solution.py
@@ -7,6 +7,13 @@
 MAP_SIDE = 8
 LOGIT_SCALE = 14.0
 EPSILON = 1e-06
+
+
+def exchange_gather(array, name, dim):
+    n_dev = lax.axis_size(name)
+    blocks = jnp.stack([array for _ in range(n_dev)])
+    blocks = lax.all_to_all(blocks, name, split_axis=0, concat_axis=0)
+    return jnp.concatenate(blocks, axis=dim)
 
 
 def depthwise(padded, weight):
@@ -55,7 +62,7 @@
     text_f = text_float * text_scale
     text_unit = text_f.astype(jnp.bfloat16)
     image_all, text_all = (
-        lax.all_gather(image_unit, ("dp", "fsdp"), axis=0, tiled=True),
+        exchange_gather(image_unit, ("dp", "fsdp"), 0),
         lax.all_gather(text_unit, ("dp", "fsdp"), axis=0, tiled=True),
     )
     local_count = images.shape[0]

time: 2230 us -> 1510 us (0.68)
  waiting for transfers between devices: 1720 us -> 983 us
  starting transfers between devices: 9.36 us -> 32 us
    all_gather x1 -> x0, waiting for transfers between devices: 749 us -> none  [local(): lax.all_gather(image_unit, ('dp', 'fsdp'), axis=0, tiled=True)]
    all_to_all x0 -> x1, starting transfers between devices: none -> 22.7 us  [exchange_gather(): blocks = lax.all_to_all(blocks, name, split_axis=0, concat_axis=0)]
    unnamed x6 -> x5, waiting for transfers between devices: 71.6 us -> 71.8 us
  transfers between devices with their start and end apart: 6 -> 6, of which waited for: 5 -> 4; matrix products, arithmetic and copies ran while one was open for 2% -> 3% of each run, Pallas kernels for 0% -> 0%
where the time goes in v1:
time: 1510 us
  waiting for transfers between devices  983 us (65%)
  blocking collectives  399 us (26%)
  other arithmetic  47.6 us (3%)
  starting transfers between devices  32 us (2%)
  local copies, waits for them, and re-layouts  20 us (1%)
  between operations  19.5 us (1%)
    all_gather x1, waiting for transfers between devices, local(): lax.all_gather(text_unit, ('dp', 'fsdp'), axis=0, tiled=True)  768 us
    unnamed x3, blocking collectives  227 us
    psum x1, waiting for transfers between devices, local(): lax.psum((part_weight, part_bias, part_block, part_head, proj_grad), 'dp')  142 us
    psum x1, blocking collectives, local(): lax.psum((part_weight, part_bias, part_block, part_head, proj_grad), 'dp')  123 us
    unnamed x5, waiting for transfers between devices  71.8 us
  transfers between devices with their start and end apart: 6, of which 4 were waited for; matrix products, arithmetic and copies ran while one was open for 3% of the time, Pallas kernels for 0%

profile of v1, /device:TPU:4, one launch (start us, length us, event | category | flops | bytes accessed | tf_op | source)
XLA Modules:
  0.0 1514.1 jit_solution(13739329893725585453)
XLA Ops:
  7.2 0.7 all-gather.6.cloned.1.call-update
  7.9 28.4 %all-gather = f32[16,192,49]{1,2,0:T(8,128)S(1)} all-gather(f32[1,192,49]{1,2,0:T(8,128)} %bitcast.226), channel_id=1, replica_groups=mesh['dp'=32,'fsdp'=16] {'fsdp'}, dimensions={0}, use_global_device_ids=true | all-gather | bytes 639744 | tf_op jit(solution)/shard_map/all_gather | solution.py:36
  36.3 0.3 copy.21
  36.6 1.2 reshape.187
  38.0 0.6 fusion.135
  39.2 0.3 dynamic-update-slice
  39.5 0.3 dynamic-update-slice.1
  39.8 0.3 dynamic-update-slice.2
  40.0 62.8 %all-reduce.14 = (f32[3072]{0:T(1024)}, f32[3072]{0:T(1024)}, f32[3072]{0:T(1024)S(1)}) all-reduce(f32[3072]{0:T(1024)S(1)} %dynamic-update-slice, f32[3072]{0:T(1024)S(1)} %dynamic-update-slice.1, f32[3072]{0:T(1024)S(1)} %dynamic-update-slice.2), channel_id=1, replica_groups=mesh['dp'=32,'fsdp'=16] {'fsdp'}, use_global_device_ids=true, to_apply=%add.2 | all-reduce | flops 9216 | bytes 73728
  102.9 0.2 fusion.133
  103.5 14.5 fusion.131
  118.3 0.3 multiply_reduce_fusion.51
  118.6 0.8 copy-done.3
  119.4 0.5 add_reduce_fusion
  119.8 1.2 broadcast_multiply_fusion.2
  121.1 0.8 div.46
  121.9 0.7 mul.1444
  122.6 0.7 broadcast_multiply_fusion.9
  123.3 0.2 multiply_reduce_fusion.54
  123.5 0.8 multiply_convert_fusion
  124.3 0.6 copy.22
  124.9 9.2 all-to-all-start.1
  134.2 2.6 multiply_reduce_fusion.58
  136.9 1.3 multiply_reduce_fusion.57
  138.2 0.7 all-to-all-done.1
  138.9 1.5 stack.102
  140.4 22.7 %all-to-all-start = ((bf16[512,2,512]{2,1,0:T(2,128)(2,1)}), bf16[512,2,512]{2,1,0:T(2,128)(2,1)}, u32[]{:S(2)}, u32[]{:S(2)}) async-start(bf16[512,2,512]{2,1,0:T(2,128)(2,1)} %stack.102), calls=%async_computation | async-start | bytes 2097152 | tf_op jit(solution)/shard_map/all_to_all | solution.py:15
  163.1 0.7 all-gather.8.cloned.1.call-update
  164.5 0.6 iota_add_fusion
  165.1 0.6 broadcast_multiply_fusion.3
  165.7 0.6 all_to_all.18
  166.4 0.7 multiply_dynamic-update-slice_fusion
  167.1 767.8 %all-gather.8.cloned.1.call-done = bf16[512,2,512]{2,1,0:T(2,128)(2,1)} async-done(((bf16[1,2,512]{2,1,0:T(2,128)(2,1)}), bf16[512,2,512]{2,1,0:T(2,128)(2,1)}) %all-gather.8.cloned.1.call-update) | async-done | bytes 1048592 | tf_op jit(solution)/shard_map/all_gather | solution.py:66
  934.9 2.3 reshape.189
  937.1 1.7 exponential_reduce_fusion.1
  938.9 0.6 fusion.137
  939.4 2.3 reshape.170
  941.7 2.3 exponential_reduce_fusion
  944.1 0.6 fusion.136
  944.6 101.5 %all-reduce.11 = (f32[1024]{0:T(1024)}, f32[1024]{0:T(1024)S(1)}, f32[1024]{0:T(1024)}) all-reduce(f32[1024]{0:T(1024)S(1)} %get-tuple-element.153, f32[1024]{0:T(1024)S(1)} %get-tuple-element.151, f32[1024]{0:T(1024)S(1)} %multiply_dynamic-update-slice_fusion), channel_id=1, replica_groups=mesh['dp'=32,'fsdp'=16] {'dp','fsdp'}, use_global_device_ids=true, to_apply=%add.5 | all-reduce | flops 3072 | bytes 24576
  1046.1 1.7 multiply_reduce_fusion.56
  1047.8 0.7 multiply_convert_fusion.3
  1048.6 3.4 multiply_reduce_fusion.52
  1052.0 0.2 fusion.129
  1052.3 1.1 multiply_reduce_fusion
  1053.4 4.7 multiply_reduce_fusion.1
  1058.1 2.4 fusion.128
  1060.7 3.8 multiply_reduce_fusion.19
  1064.6 21.1 %all-gather.2 = bf16[16,2,512]{2,1,0:T(2,128)(2,1)S(1)} all-gather(bf16[1,2,512]{2,1,0:T(2,128)(2,1)S(1)} %bitcast.276), channel_id=1, replica_groups=mesh['dp'=32,'fsdp'=16] {'fsdp'}, dimensions={0}, use_global_device_ids=true | all-gather | bytes 34816 | tf_op jit(solution)/shard_map/all_gather | solution.py:107
  1085.7 62.4 %all-reduce.13 = (f32[3072]{0:T(1024)S(1)}, f32[3072]{0:T(1024)S(1)}, f32[3072]{0:T(1024)S(1)}) all-reduce(f32[3072]{0:T(1024)S(1)} %get-tuple-element.58, f32[3072]{0:T(1024)S(1)} %copy-done.74, f32[3072]{0:T(1024)S(1)} %copy-done.73), channel_id=3, replica_groups=mesh['dp'=32,'fsdp'=16] {'fsdp'}, use_global_device_ids=true, to_apply=%region_70.71.clone | all-reduce | flops 9216 | bytes 73728
  1148.5 0.9 stack.152
  1149.4 1.7 copy.23
  1151.4 1.4 reduce_sum.649
  1152.8 1.0 fusion.138
  1154.1 9.5 fusion.97
  1163.6 0.6 reduce_sum.647
  1165.5 0.6 reduce_sum.651
  1166.8 0.4 fusion.113
  1167.2 0.7 fusion.115
  1167.9 70.4 %reduce-scatter.4.cloned.1.call-done = f32[192,49]{1,0:T(8,128)} async-done(((f32[3072,49]{1,0:T(8,128)}), f32[192,49]{1,0:T(8,128)}) %reduce-scatter.4.cloned.1.call-update) | async-done | bytes 37648
  1238.3 1.0 copy.24
  1239.3 123.1 %all-reduce.12 = (f32[49,192]{1,0:T(8,128)}, f32[192]{0:T(256)}, f32[192]{0:T(256)}, f32[192]{0:T(256)}) all-reduce(f32[49,192]{1,0:T(8,128)S(1)} %copy.24, f32[192]{0:T(256)S(1)} %dynamic-slice.4, f32[192]{0:T(256)S(1)} %dynamic-slice.6, f32[192]{0:T(256)S(1)} %dynamic-slice.8), channel_id=1, replica_groups=mesh['dp'=32,'fsdp'=16] {'dp'}, use_global_device_ids=true, to_apply=%region_68.69 | all-reduce | flops 9984 | bytes 79872 | tf_op jit(solution)/shard_map/psum | solution.py:147
  1362.4 142.3 %all-reduce.17.cloned.1.call-done = f32[192,512]{1,0:T(8,128)} async-done(((f32[192,512]{1,0:T(8,128)}), f32[192,512]{1,0:T(8,128)}) %all-reduce.17.cloned.1.call-update) | async-done | bytes 393232 | tf_op jit(solution)/shard_map/psum | solution.py:147
  1504.6 1.8 copy.35
  (225 shorter events, 1.6 us)
Async XLA Ops:
  7.2 127.1 %all-gather.6.cloned.1.call-start = ((), (), s32[]{:S(2)}) async-start(), calls=%async_computation.3 | async-start | bytes 3342336 | tf_op jit(solution)/shard_map/all_gather | solution.py:55
  37.8 65.1 %copy-start.6 = (f32[3072,49]{0,1:T(8,128)S(1)}, f32[3072,49]{0,1:T(8,128)}, u32[]{:S(2)}) copy-start(f32[3072,49]{0,1:T(8,128)} %reshape.187) | copy-start | bytes 1806340
  103.1 14.9 copy-start.7
  103.1 14.9 copy-start.9
  103.1 14.9 copy-start.11
  103.1 14.9 copy-start.13
  103.3 14.7 copy-start.15
  103.3 14.7 copy-start.17
  103.3 14.7 copy-start.19
  103.4 14.7 copy-start.21
  103.4 14.7 copy-start.23
  103.4 14.7 copy-start.25
  103.4 14.7 copy-start.27
  103.4 14.7 copy-start.29
  103.4 14.7 copy-start.31
  103.4 14.7 copy-start.33
  103.4 14.7 copy-start.35
  103.4 14.7 copy-start.37
  103.4 14.7 copy-start.39
  103.5 14.7 copy-start.41
  103.5 14.7 copy-start.43
  103.5 14.7 copy-start.45
  103.5 14.7 copy-start.47
  103.5 14.7 copy-start.49
  103.5 14.7 copy-start.51
  118.6 15.5 %copy-start.77 = (bf16[2,512]{1,0:T(2,128)(2,1)S(1)}, bf16[2,512]{1,0:T(2,128)(2,1)}, u32[]{:S(2)}) copy-start(bf16[2,512]{1,0:T(2,128)(2,1)} %param.13) | copy-start | bytes 6148
  124.9 14.0 all-to-all-start.1
  138.9 26.3 %copy-start.72 = (f32[3072]{0:T(1024)S(1)}, f32[3072]{0:T(1024)}, u32[]{:S(2)}) copy-start(f32[3072]{0:T(1024)} %get-tuple-element.86) | copy-start | bytes 36868
  140.4 799.1 %all-to-all-start = ((bf16[512,2,512]{2,1,0:T(2,128)(2,1)}), bf16[512,2,512]{2,1,0:T(2,128)(2,1)}, u32[]{:S(2)}, u32[]{:S(2)}) async-start(bf16[512,2,512]{2,1,0:T(2,128)(2,1)} %stack.102), calls=%async_computation | async-start | bytes 2097152 | tf_op jit(solution)/shard_map/all_to_all | solution.py:15
  163.1 771.8 %all-gather.8.cloned.1.call-start = ((), (), s32[]{:S(2)}) async-start(), calls=%async_computation.5 | async-start | bytes 1050624 | tf_op jit(solution)/shard_map/all_gather | solution.py:66
  163.8 1074.5 %reduce-scatter.4.cloned.1.call-start = ((), (), s32[]{:S(2)}) async-start(), calls=%async_computation.6 | async-start | bytes 1671168
  937.1 4.6 copy-start.76
  941.7 106.8 %copy-start.81 = (f32[2]{0:T(128)S(1)}, f32[2]{0:T(128)}, u32[]{:S(2)}) copy-start(f32[2]{0:T(128)} %copy-done.80) | copy-start | bytes 28
  941.7 106.8 %copy-start.84 = (f32[2]{0:T(128)S(1)}, f32[2]{0:T(128)}, u32[]{:S(2)}) copy-start(f32[2]{0:T(128)} %copy-done.83) | copy-start | bytes 28
  1048.5 3.5 copy-start.75
  1053.4 4.8 copy-start.4
  1060.5 25.2 %copy-start.73 = (f32[3072]{0:T(1024)S(1)}, f32[3072]{0:T(1024)}, u32[]{:S(2)}) copy-start(f32[3072]{0:T(1024)} %get-tuple-element.72) | copy-start | bytes 36868
  1060.5 25.1 %copy-start.74 = (f32[3072]{0:T(1024)S(1)}, f32[3072]{0:T(1024)}, u32[]{:S(2)}) copy-start(f32[3072]{0:T(1024)} %get-tuple-element.56) | copy-start | bytes 36868
  1060.5 87.8 %copy-start.54 = (f32[3072]{0:T(1024)S(1)}, f32[3072]{0:T(1024)}, u32[]{:S(2)}) copy-start(f32[3072]{0:T(1024)} %get-tuple-element.9) | copy-start | bytes 36868
  1060.6 87.8 %copy-start.55 = (f32[3072]{0:T(1024)S(1)}, f32[3072]{0:T(1024)}, u32[]{:S(2)}) copy-start(f32[3072]{0:T(1024)} %get-tuple-element.10) | copy-start | bytes 36868
  1060.6 87.8 %copy-start.56 = (f32[3072]{0:T(1024)S(1)}, f32[3072]{0:T(1024)}, u32[]{:S(2)}) copy-start(f32[3072]{0:T(1024)} %get-tuple-element.11) | copy-start | bytes 36868
  1060.6 87.8 %copy-start.57 = (f32[3072]{0:T(1024)S(1)}, f32[3072]{0:T(1024)}, u32[]{:S(2)}) copy-start(f32[3072]{0:T(1024)} %get-tuple-element.12) | copy-start | bytes 36868
  1060.6 87.8 %copy-start.58 = (f32[3072]{0:T(1024)S(1)}, f32[3072]{0:T(1024)}, u32[]{:S(2)}) copy-start(f32[3072]{0:T(1024)} %get-tuple-element.13) | copy-start | bytes 36868
  1060.6 87.8 %copy-start.59 = (f32[3072]{0:T(1024)S(1)}, f32[3072]{0:T(1024)}, u32[]{:S(2)}) copy-start(f32[3072]{0:T(1024)} %get-tuple-element.14) | copy-start | bytes 36868
  1060.6 87.8 %copy-start.60 = (f32[3072]{0:T(1024)S(1)}, f32[3072]{0:T(1024)}, u32[]{:S(2)}) copy-start(f32[3072]{0:T(1024)} %get-tuple-element.15) | copy-start | bytes 36868
  1060.6 87.8 %copy-start.61 = (f32[3072]{0:T(1024)S(1)}, f32[3072]{0:T(1024)}, u32[]{:S(2)}) copy-start(f32[3072]{0:T(1024)} %get-tuple-element.16) | copy-start | bytes 36868
  1060.6 87.8 %copy-start.62 = (f32[3072]{0:T(1024)S(1)}, f32[3072]{0:T(1024)}, u32[]{:S(2)}) copy-start(f32[3072]{0:T(1024)} %get-tuple-element.17) | copy-start | bytes 36868
  1060.6 87.8 %copy-start.63 = (f32[3072]{0:T(1024)S(1)}, f32[3072]{0:T(1024)}, u32[]{:S(2)}) copy-start(f32[3072]{0:T(1024)} %get-tuple-element.18) | copy-start | bytes 36868
  1060.6 87.8 %copy-start.64 = (f32[3072]{0:T(1024)S(1)}, f32[3072]{0:T(1024)}, u32[]{:S(2)}) copy-start(f32[3072]{0:T(1024)} %get-tuple-element.19) | copy-start | bytes 36868
  1060.7 87.8 %copy-start.65 = (f32[3072]{0:T(1024)S(1)}, f32[3072]{0:T(1024)}, u32[]{:S(2)}) copy-start(f32[3072]{0:T(1024)} %get-tuple-element.20) | copy-start | bytes 36868
  1060.7 87.8 %copy-start.66 = (f32[3072]{0:T(1024)S(1)}, f32[3072]{0:T(1024)}, u32[]{:S(2)}) copy-start(f32[3072]{0:T(1024)} %get-tuple-element.21) | copy-start | bytes 36868
  1060.7 87.8 %copy-start.67 = (f32[3072]{0:T(1024)S(1)}, f32[3072]{0:T(1024)}, u32[]{:S(2)}) copy-start(f32[3072]{0:T(1024)} %get-tuple-element.22) | copy-start | bytes 36868
  1060.7 87.8 %copy-start.68 = (f32[3072]{0:T(1024)S(1)}, f32[3072]{0:T(1024)}, u32[]{:S(2)}) copy-start(f32[3072]{0:T(1024)} %get-tuple-element.23) | copy-start | bytes 36868
  1060.7 87.8 %copy-start.69 = (f32[3072]{0:T(1024)S(1)}, f32[3072]{0:T(1024)}, u32[]{:S(2)}) copy-start(f32[3072]{0:T(1024)} %get-tuple-element.24) | copy-start | bytes 36868
  1060.7 87.8 %copy-start.70 = (f32[3072]{0:T(1024)S(1)}, f32[3072]{0:T(1024)}, u32[]{:S(2)}) copy-start(f32[3072]{0:T(1024)} %get-tuple-element.25) | copy-start | bytes 36868
  1151.3 353.3 %all-reduce.17.cloned.1.call-start = ((), (), s32[]{:S(2)}) async-start(), calls=%async_computation.4 | async-start | bytes 786432 | tf_op jit(solution)/shard_map/psum | solution.py:147
  1154.0 9.6 copy-start.85
  1154.0 11.5 copy-start.86
  1154.0 12.8 copy-start.5
  1154.0 12.8 copy-start.79
  1154.0 12.8 copy-start.82
  1154.0 12.8 copy-start.89
  1154.0 12.8 copy-start.95
  1154.1 12.8 copy-start.96
  (39 other events, 92.7 us)
Sparse Core Ops, SparseCore 0:
  11.3 68.0 all-gather.5
  166.6 768.2 all-gather.7
  1151.4 86.8 reduce-scatter.3
  1241.7 262.9 all-reduce.16
